TPU v7x, 256 devices: a whole 4x4x8 slice. The times are simulated.
256 devices in a mesh: dp: 4 (over y_hi, core), seq: 8 (over z), head: 8 (over x, y_lo).
Axes of the slice: x: 4, y: 4 (y_hi: 2, y_lo: 2; y = y_hi * 2 + y_lo), z: 8, core: 2. Of those that a mesh axis runs over, the one named last changes fastest.
Arguments:
- tokens: bfloat16 [4, 8192, 512], P('dp', ('seq', 'head')), may hold values from -800 to 800
- bin_ids: int32 [4, 8192], P('dp'), may hold values from 0 to 127, never falling along the last dimension, each value on 1 to 256 neighbouring positions
- pattern: int32 [4, 64, 9], P('dp'), may hold values from 0 to 63, as said below
- w_qkv: bfloat16 [512, 1536], replicated, may hold values from -3.2 to 3.2
- w_out: bfloat16 [512, 512], replicated, may hold values from -5 to 5
- head_bias: float32 [8], replicated, may hold values from -3 to 400
- grad_output: bfloat16 [4, 8192, 512], P('dp', ('seq', 'head')), may hold values from -6 to 6
Outputs:
- output: bfloat16 [4, 8192, 512], P('dp', ('seq', 'head'))
- grad_tokens: bfloat16 [4, 8192, 512], P('dp', ('seq', 'head'))
- grad_w_qkv: float32 [512, 1536], P(None, 'head')
- grad_w_out: float32 [512, 512], P('head')
Inputs may be any that keep to these rules, and one draw needn't show every extreme that they name: `pattern`: row i of sequence b lists (i + o) mod 64 for the 9 offsets o of sequence b, in the same order in every row: 0, 1, -1, then distinct a from 2 to 31, then their negatives. So block J is in row I exactly when I is in row J. `bin_ids`: bin numbers never fall along a sequence.
All inputs are finite; a program needn't handle non-finite values.
Results may differ from a plain program's by a relative error of at most 0.01.
Values may be sent and summed in bfloat16 or wider, within the bound.
A program may use at most 64 MiB of HBM per device.

v0:
```python
import math
import jax
import jax.numpy as jnp
from jax import lax
from jax.sharding import PartitionSpec as P

D = 512
HEADS = 8
HD = 64
BLK = 128
NNZ = 9
EPSILON = 1e-05


def normalize(token_rows):
    widened = token_rows.astype(jnp.float32)
    spread = jnp.sqrt(jnp.mean(widened * widened, axis=-1, keepdims=True) + EPSILON)
    return (widened / spread, spread)


def query_scores(query_blk, key_blk, bin_query, bin_key, bias_local, factor):
    raw_scores = jnp.einsum(
        "gqhe,gnkhe->ghqnk", query_blk, key_blk, preferred_element_type=jnp.float32
    )
    same_bin = (bin_query[:, None, :, None, None] == bin_key[:, None, None, :, :]).astype(
        jnp.float32
    )
    scores = raw_scores * factor + bias_local[None, :, None, None, None] * same_bin
    return scores.reshape(scores.shape[0], scores.shape[1], scores.shape[2], -1)


def body(tokens, bin_ids, pattern, w_qkv, w_out, head_bias, grad_output):
    tok_rows = tokens.shape[1]
    head_parts = lax.axis_size("head")
    local_heads = HEADS // head_parts
    seq_rows = tok_rows * head_parts
    seq_length = bin_ids.shape[1]
    blocks_all = seq_length // BLK
    local_blocks = seq_rows // BLK
    group_size = math.gcd(local_blocks, 4)
    group_count = local_blocks // group_size
    factor = 1.0 / math.sqrt(HD)
    seq_pos = lax.axis_index("seq")
    head_pos = lax.axis_index("head")
    first_block = seq_pos * local_blocks
    key_lists = lax.dynamic_slice_in_dim(pattern[0], first_block, local_blocks, 0)
    bin_table = bin_ids[0].reshape(blocks_all, BLK)
    bin_local = lax.dynamic_slice_in_dim(bin_table, first_block, local_blocks, 0)
    bias_local = lax.dynamic_slice_in_dim(head_bias, head_pos * local_heads, local_heads, 0)

    def grouped(array):
        return array.reshape((group_count, group_size) + array.shape[1:])

    normed, spread = normalize(tokens[0])
    hidden = normed.astype(jnp.bfloat16)
    packed = jnp.dot(hidden, w_qkv, preferred_element_type=jnp.float32).astype(jnp.bfloat16)
    packed = packed.reshape(tok_rows, HEADS, 3 * HD)
    packed_heads = lax.all_to_all(packed, "head", split_axis=1, concat_axis=0, tiled=True)
    queries = packed_heads[:, :, :HD]
    pair_local = packed_heads[:, :, HD:]
    pair_all = lax.all_gather(pair_local, "seq", axis=0, tiled=True)
    pair_table = pair_all.reshape(blocks_all, BLK, local_heads, 2 * HD)
    query_blocks = queries.reshape(local_blocks, BLK, local_heads, HD)

    def forward_group(entries):
        query_blk, key_rows, bin_query = entries
        pair_blk = jnp.take(pair_table, key_rows, axis=0)
        bin_key = jnp.take(bin_table, key_rows, axis=0)
        scores = query_scores(query_blk, pair_blk[..., :HD], bin_query, bin_key, bias_local, factor)
        row_max = jnp.max(scores, axis=-1, keepdims=True)
        log_total = row_max + jnp.log(jnp.sum(jnp.exp(scores - row_max), axis=-1, keepdims=True))
        probs = jnp.exp(scores - log_total).astype(jnp.bfloat16)
        value_flat = pair_blk[..., HD:].reshape(group_size, NNZ * BLK, local_heads, HD)
        attended = jnp.einsum(
            "ghqm,gmhe->gqhe", probs, value_flat, preferred_element_type=jnp.float32
        )
        return (attended.astype(jnp.bfloat16), log_total[..., 0])

    attended, log_blocks = lax.map(
        forward_group, (grouped(query_blocks), grouped(key_lists), grouped(bin_local))
    )
    attended_heads = attended.reshape(seq_rows, local_heads, HD)
    log_blocks = log_blocks.reshape(local_blocks, local_heads, BLK)
    attended_tok = lax.all_to_all(
        attended_heads, "head", split_axis=0, concat_axis=1, tiled=True
    ).reshape(tok_rows, D)
    result = jnp.dot(attended_tok, w_out, preferred_element_type=jnp.float32).astype(jnp.bfloat16)
    grad_rows = grad_output[0]
    grad_att = jnp.dot(grad_rows, w_out.T, preferred_element_type=jnp.float32).astype(jnp.bfloat16)
    grad_heads = lax.all_to_all(
        grad_att.reshape(tok_rows, HEADS, HD), "head", split_axis=1, concat_axis=0, tiled=True
    )
    delta_rows = jnp.sum(
        grad_heads.astype(jnp.float32) * attended_heads.astype(jnp.float32), axis=-1
    )
    delta_blocks = delta_rows.reshape(local_blocks, BLK, local_heads).swapaxes(1, 2)
    grad_blocks = grad_heads.reshape(local_blocks, BLK, local_heads, HD)

    def query_core(entries):
        query_blk, grad_blk, log_blk, delta_blk, key_rows, bin_query = entries
        pair_blk = jnp.take(pair_table, key_rows, axis=0)
        bin_key = jnp.take(bin_table, key_rows, axis=0)
        scores = query_scores(query_blk, pair_blk[..., :HD], bin_query, bin_key, bias_local, factor)
        probs = jnp.exp(scores - log_blk[..., None])
        value_flat = pair_blk[..., HD:].reshape(group_size, NNZ * BLK, local_heads, HD)
        key_flat = pair_blk[..., :HD].reshape(group_size, NNZ * BLK, local_heads, HD)
        grad_prob = jnp.einsum(
            "gqhe,gmhe->ghqm", grad_blk, value_flat, preferred_element_type=jnp.float32
        )
        grad_score = (probs * (grad_prob - delta_blk[..., None]) * factor).astype(jnp.bfloat16)
        grad_query = jnp.einsum(
            "ghqm,gmhe->gqhe", grad_score, key_flat, preferred_element_type=jnp.float32
        )
        return (grad_query.astype(jnp.bfloat16), grad_score, probs)

    query_entries = (
        grouped(query_blocks),
        grouped(grad_blocks),
        grouped(log_blocks),
        grouped(delta_blocks),
        grouped(key_lists),
        grouped(bin_local),
    )

    def scatter_step(carried, entries):
        query_blk, grad_blk = (entries[0], entries[1])
        key_rows = entries[4]
        grad_query, grad_score, probs = query_core(entries)
        key_part = jnp.einsum(
            "ghqm,gqhe->gmhe", grad_score, query_blk, preferred_element_type=jnp.float32
        )
        value_part = jnp.einsum(
            "ghqm,gqhe->gmhe",
            probs.astype(jnp.bfloat16),
            grad_blk,
            preferred_element_type=jnp.float32,
        )
        both_parts = jnp.concatenate([key_part, value_part], axis=-1)
        both_parts = both_parts.reshape(group_size * NNZ, BLK, local_heads, 2 * HD)
        carried = carried.at[key_rows.reshape(-1)].add(both_parts)
        return (carried, grad_query)

    empty_sum = jnp.zeros((blocks_all, BLK, local_heads, 2 * HD), jnp.float32)
    pair_sums, grad_queries = lax.scan(scatter_step, empty_sum, query_entries)
    own_pairs = lax.psum_scatter(
        pair_sums.reshape(seq_length, local_heads, 2 * HD), "seq", scatter_dimension=0, tiled=True
    )
    grad_pairs = own_pairs.astype(jnp.bfloat16)
    grad_packed_heads = jnp.concatenate(
        [grad_queries.reshape(seq_rows, local_heads, HD), grad_pairs], axis=-1
    )
    grad_packed = lax.all_to_all(
        grad_packed_heads, "head", split_axis=0, concat_axis=1, tiled=True
    ).reshape(tok_rows, 3 * D)
    grad_hidden = jnp.dot(grad_packed, w_qkv.T, preferred_element_type=jnp.float32)
    inner = jnp.mean(grad_hidden * normed, axis=-1, keepdims=True)
    grad_input = ((grad_hidden - normed * inner) / spread).astype(jnp.bfloat16)
    local_qkv = jnp.einsum("td,tc->dc", hidden, grad_packed, preferred_element_type=jnp.float32)
    local_out = jnp.einsum("td,tc->dc", grad_rows, attended_tok, preferred_element_type=jnp.float32)
    total_qkv, total_out = lax.psum((local_qkv, local_out), ("dp", "seq", "head"))
    own_qkv = lax.dynamic_slice_in_dim(
        total_qkv, head_pos * local_heads * 3 * HD, local_heads * 3 * HD, 1
    )
    own_out = lax.dynamic_slice_in_dim(total_out, head_pos * local_heads * HD, local_heads * HD, 1)
    return (result[None], grad_input[None], own_qkv, own_out.T)


def solution(mesh):
    return jax.shard_map(
        body,
        mesh=mesh,
        in_specs=(
            P("dp", ("seq", "head"), None),
            P("dp", None),
            P("dp", None, None),
            P(),
            P(),
            P(),
            P("dp", ("seq", "head"), None),
        ),
        out_specs=(
            P("dp", ("seq", "head"), None),
            P("dp", ("seq", "head"), None),
            P(None, "head"),
            P("head", None),
        ),
        check_vma=False,
    )
```

profile of v0, /device:TPU:2, one launch (start us, length us, event | category | flops | bytes accessed | tf_op | source)
XLA Modules:
  0.0 558.7 jit_solution(6286347255980764140)
XLA Ops:
  10.6 12.6 %all_to_all.63 = bf16[128,8,192]{0,2,1:T(8,128)(2,1)S(1)} all-to-all(bf16[128,8,192]{0,2,1:T(8,128)(2,1)S(1)} %bitcast.271), channel_id=1, replica_groups=mesh['dp'=4,'seq'=8,'head'=8] {'head'}, dimensions={1} | all-to-all | bytes 786432 | tf_op jit(solution)/shard_map/all_to_all | solution.py:58
  25.1 4.8 all-to-all-start.2
  30.9 36.5 %all-gather.2.cloned.1.call-done = bf16[8192,1,128]{0,2,1:T(8,128)(2,1)} async-done(((bf16[1024,1,128]{0,2,1:T(8,128)(2,1)}), bf16[8192,1,128]{0,2,1:T(8,128)(2,1)}) %all-gather.2.cloned.1.call-update) | async-done | bytes 2097168 | tf_op jit(solution)/shard_map/all_gather | solution.py:61
  67.4 4.1 copy.119
  72.1 40.3 %while.24 = (s32[]{:T(128)}, bf16[2,4,128,1,64]{2,4,1,3,0:T(8,128)(2,1)}, f32[2,4,1,128]{3,1,2,0:T(4,128)}, s32[2,4,9]{2,1,0:T(4,128)S(1)}, bf16[64,128,1,128]{3...) while((s32[]{:T(128)}, ...), condition=%wide.region_4.7_spmd, body=%wide.region_1.6_spmd.sunk | while | flops 156931296 | bytes 39141280 | solution.py:79
  73.5 3.4 gather_fusion
  80.7 3.7 fusion.80
  86.2 3.1 copy.153
  93.6 3.4 gather_fusion
  100.8 3.7 fusion.80
  106.3 3.1 copy.153
  114.1 2.5 broadcast_in_dim.54
  116.5 86.1 %while.25 = (s32[]{:T(128)}, f32[64,128,1,128]{3,1,0,2:T(8,128)}, bf16[2,4,128,1,64]{2,4,1,3,0:T(8,128)(2,1)}, s32[2,4,9]{2,1,0:T(4,128)S(1)}, bf16[2,4,128,1,64...) while((s32[]{:T(128)}, f32[64,128,1,128]{3,1,0,2:T(8,128)}, ...), condition=%wide.region_8.11_spmd, body=%wide.region_6.10_spmd.sunk | while | flops 385783744 | bytes 64560684 | solution.py:144
  119.2 2.4 gather_fusion.3
  128.3 2.5 copy.158
  133.0 4.2 select_add_fusion.3
  137.2 3.1 copy.155
  140.3 2.5 fusion.94
  146.5 3.1 copy.157
  149.6 10.0 %scatter_fusion = f32[64,128,128]{2,1,0:T(8,128)} fusion(f32[64,128,128]{2,1,0:T(8,128)} %bitcast.263, s32[36]{0:T(128)S(1)} %copy-done.24, f32[36,128,128]{2,1,0:T(8,128)} %bitcast.257), kind=kCustom, calls=%fused_computation.4.clone.1 | custom fusion | flops 589824 | bytes 7078032 | tf_op jit(solution)/shard_map/while/body/eval_jaxpr/scatter-add | solution.py:140
  171.3 2.5 copy.158
  176.0 4.2 select_add_fusion.3
  180.2 3.1 copy.155
  183.3 2.5 fusion.94
  189.4 3.1 copy.157
  192.5 10.0 %scatter_fusion = f32[64,128,128]{2,1,0:T(8,128)} fusion(f32[64,128,128]{2,1,0:T(8,128)} %bitcast.263, s32[36]{0:T(128)S(1)} %copy-done.24, f32[36,128,128]{2,1,0:T(8,128)} %bitcast.257), kind=kCustom, calls=%fused_computation.4.clone.1 | custom fusion | flops 589824 | bytes 7078032 | tf_op jit(solution)/shard_map/while/body/eval_jaxpr/scatter-add | solution.py:140
  207.7 5.7 %all-to-all-start.1 = ((bf16[8,2,4096]{2,1,0:T(2,128)(2,1)}), bf16[8,2,4096]{2,1,0:T(2,128)(2,1)S(1)}, u32[]{:S(2)}, u32[]{:S(2)}) async-start(bf16[8,2,4096]{2,1,0:T(2,128)(2,1)} %reshape.393), calls=%async_computation.1 | async-start | bytes 262144 | tf_op jit(solution)/shard_map/all_to_all | solution.py:84
  213.8 43.0 %reduce-scatter.2.cloned.1.call-done = f32[1024,1,128]{2,1,0:T(1,128)} async-done(((f32[8192,1,128]{2,1,0:T(1,128)}), f32[1024,1,128]{2,1,0:T(1,128)}) %reduce-scatter.2.cloned.1.call-update) | async-done | bytes 524304 | tf_op jit(solution)/shard_map/reduce_scatter | solution.py:145
  260.2 4.1 reduce.10
  265.6 5.7 %all-to-all-start.3 = ((bf16[8,2,12288]{2,1,0:T(2,128)(2,1)}), bf16[8,2,12288]{2,1,0:T(2,128)(2,1)S(1)}, u32[]{:S(2)}, u32[]{:S(2)}) async-start(bf16[8,2,12288]{2,1,0:T(2,128)(2,1)} %reshape.395), calls=%async_computation.4 | async-start | bytes 786432 | tf_op jit(solution)/shard_map/all_to_all | solution.py:152
  273.3 4.7 all-to-all-done.3
  285.3 263.5 %all-reduce.3.cloned.1.call-done = (f32[512,1536]{0,1:T(8,128)}, f32[512,512]{0,1:T(8,128)}) async-done(((f32[512,1536]{0,1:T(8,128)}, f32[512,512]{0,1:T(8,128)}), (f32[512,1536]{0,1:T(8,128)}, f32[512,512]{0,1:T(8,128)})) %all-reduce.3.cloned.1.call-update) | async-done | bytes 4194320 | tf_op jit(solution)/shard_map/psum | solution.py:160
  (216 shorter events, 83.3 us)
Async XLA Ops:
  7.2 60.2 %all-gather.2.cloned.1.call-start = ((), (), s32[]{:S(2)}) async-start(), calls=%async_computation.5 | async-start | bytes 2359296 | tf_op jit(solution)/shard_map/all_gather | solution.py:61
  9.0 15.1 %copy-start.6 = (bf16[512,512]{1,0:T(8,128)(2,1)S(1)}, bf16[512,512]{1,0:T(8,128)(2,1)}, u32[]{:S(2)}) copy-start(bf16[512,512]{1,0:T(8,128)(2,1)} %param.19) | copy-start | bytes 1572868
  9.0 15.1 %copy-start.17 = (bf16[1,128,512]{2,1,0:T(8,128)(2,1)S(1)}, bf16[1,128,512]{2,1,0:T(8,128)(2,1)}, u32[]{:S(2)}) copy-start(bf16[1,128,512]{2,1,0:T(8,128)(2,1)} %param.21) | copy-start | bytes 393220
  10.3 19.6 %copy-start.25 = (s32[1,64,9]{1,0,2:T(1,128)S(1)}, s32[1,64,9]{1,0,2:T(1,128)}, u32[]{:S(2)}) copy-start(s32[1,64,9]{1,0,2:T(1,128)} %param.17) | copy-start | bytes 6916
  10.4 19.8 %copy-start.28 = (f32[8]{0:T(128)S(1)}, f32[8]{0:T(128)}, u32[]{:S(2)}) copy-start(f32[8]{0:T(128)} %param.20) | copy-start | bytes 100
  10.4 20.4 %copy-start.3 = (s32[1,8192]{1,0:T(1,128)S(1)}, s32[1,8192]{1,0:T(1,128)}, u32[]{:S(2)}) copy-start(s32[1,8192]{1,0:T(1,128)} %param.16) | copy-start | bytes 98308
  25.1 87.3 %all-to-all-start.2 = ((bf16[128,8,64]{0,2,1:T(8,128)(2,1)}), bf16[128,8,64]{0,2,1:T(8,128)(2,1)S(1)}, u32[]{:S(2)}, u32[]{:S(2)}) async-start(bf16[128,8,64]{0,2,1:T(8,128)(2,1)} %bitcast.50), calls=%async_computation.2 | async-start | bytes 262144 | tf_op jit(solution)/shard_map/all_to_all | solution.py:90
  29.9 226.8 %reduce-scatter.2.cloned.1.call-start = ((), (), s32[]{:S(2)}) async-start(), calls=%async_computation.6 | async-start | bytes 4718592 | tf_op jit(solution)/shard_map/reduce_scatter | solution.py:145
  80.7 5.4 copy-start.22
  86.1 3.2 copy-start.23
  86.1 3.1 copy-start.10
  100.8 5.4 copy-start.22
  106.3 3.2 copy-start.23
  106.3 3.1 copy-start.10
  116.5 2.6 copy-start.20
  116.5 6.5 %copy-start.8 = (bf16[2,4,128,1,64]{2,4,1,3,0:T(8,128)(2,1)}, bf16[2,4,128,1,64]{2,4,1,3,0:T(8,128)(2,1)S(1)}, u32[]{:S(2)}) copy-start(bf16[2,4,128,1,64]{2,4,1,3,0:T(8,128)(2,1)S(1)} %get-tuple-element.496) | copy-start | bytes 393220 | tf_op jit(solution)/shard_map/while
  140.3 2.5 copy-start.1
  146.5 3.1 copy-start.24
  149.6 10.0 %copy-start.21 = (f32[2,4,1,128]{3,1,2,0:T(4,128)S(1)}, f32[2,4,1,128]{3,1,2,0:T(4,128)}, u32[]{:S(2)}) copy-start(f32[2,4,1,128]{3,1,2,0:T(4,128)} %copy-done.20) | copy-start | bytes 12292 | tf_op jit(solution)/shard_map/while
  159.5 2.6 copy-start.20
  159.5 6.5 %copy-start.8 = (bf16[2,4,128,1,64]{2,4,1,3,0:T(8,128)(2,1)}, bf16[2,4,128,1,64]{2,4,1,3,0:T(8,128)(2,1)S(1)}, u32[]{:S(2)}) copy-start(bf16[2,4,128,1,64]{2,4,1,3,0:T(8,128)(2,1)S(1)} %get-tuple-element.496) | copy-start | bytes 393220 | tf_op jit(solution)/shard_map/while
  183.3 2.5 copy-start.1
  187.5 1.9 copy-start.15
  189.4 3.1 copy-start.24
  192.5 10.0 %copy-start.21 = (f32[2,4,1,128]{3,1,2,0:T(4,128)S(1)}, f32[2,4,1,128]{3,1,2,0:T(4,128)}, u32[]{:S(2)}) copy-start(f32[2,4,1,128]{3,1,2,0:T(4,128)} %copy-done.20) | copy-start | bytes 12292 | tf_op jit(solution)/shard_map/while
  203.5 9.9 %copy-start.16 = (bf16[2,4,128,1,64]{2,4,1,3,0:T(8,128)(2,1)S(1)}, bf16[2,4,128,1,64]{2,4,1,3,0:T(8,128)(2,1)}, u32[]{:S(2)}) copy-start(bf16[2,4,128,1,64]{2,4,1,3,0:T(8,128)(2,1)} %get-tuple-element.119) | copy-start | bytes 393220
  207.7 57.9 %all-to-all-start.1 = ((bf16[8,2,4096]{2,1,0:T(2,128)(2,1)}), bf16[8,2,4096]{2,1,0:T(2,128)(2,1)S(1)}, u32[]{:S(2)}, u32[]{:S(2)}) async-start(bf16[8,2,4096]{2,1,0:T(2,128)(2,1)} %reshape.393), calls=%async_computation.1 | async-start | bytes 262144 | tf_op jit(solution)/shard_map/all_to_all | solution.py:84
  260.2 11.9 %copy-start.18 = (bf16[1,128,512]{2,1,0:T(8,128)(2,1)S(1)}, bf16[1,128,512]{2,1,0:T(8,128)(2,1)}, u32[]{:S(2)}) copy-start(bf16[1,128,512]{2,1,0:T(8,128)(2,1)} %param.21) | copy-start | bytes 393220
  265.6 12.4 %all-to-all-start.3 = ((bf16[8,2,12288]{2,1,0:T(2,128)(2,1)}), bf16[8,2,12288]{2,1,0:T(2,128)(2,1)S(1)}, u32[]{:S(2)}, u32[]{:S(2)}) async-start(bf16[8,2,12288]{2,1,0:T(2,128)(2,1)} %reshape.395), calls=%async_computation.4 | async-start | bytes 786432 | tf_op jit(solution)/shard_map/all_to_all | solution.py:152
  271.3 277.5 %all-reduce.3.cloned.1.call-start = ((), (), s32[]{:S(2)}) async-start(), calls=%async_computation.7 | async-start | bytes 8388608 | tf_op jit(solution)/shard_map/psum | solution.py:160
  273.3 6.2 %copy-start.13 = (bf16[1,128,512]{2,1,0:T(8,128)(2,1)S(1)}, bf16[1,128,512]{2,1,0:T(8,128)(2,1)}, u32[]{:S(2)}) copy-start(bf16[1,128,512]{2,1,0:T(8,128)(2,1)} %param.15) | copy-start | bytes 393220
  273.3 6.2 %copy-start.27 = (f32[128]{0:T(128)S(1)}, f32[128]{0:T(128)}, u32[]{:S(2)}) copy-start(f32[128]{0:T(128)} %copy-done.26) | copy-start | bytes 1540
  (19 other events, 21.8 us)
Sparse Core Ops, SparseCore 0:
  24.2 43.1 all-gather.1
  202.7 53.9 reduce-scatter.1
  281.9 266.7 all-reduce.2
where the time goes:
time: 561 us; the launch traced here: 559 us
  waiting for transfers between devices  348 us (62%)
  local copies, waits for them, and re-layouts  90.9 us (16%)
  other arithmetic  41.3 us (7%)
  matrix products  35.3 us (6%)
  starting transfers between devices  16.3 us (3%)
  between operations  14 us (2%)
  blocking collectives  12.6 us (2%)
    psum x1, waiting for transfers between devices, body(): lax.psum((local_qkv, local_out), ('dp', 'seq', 'head'))  264 us
    reduce_scatter x1, waiting for transfers between devices, body(): lax.psum_scatter(pair_sums.reshape(seq_length, local_heads, 2 * HD), 'seq...  43 us
    all_gather x1, waiting for transfers between devices, body(): pair_all = lax.all_gather(pair_local, 'seq', axis=0, tiled=True)  36.5 us
    scatter-add x2, other arithmetic, scatter_step(): carried = carried.at[key_rows.reshape(-1)].add(both_parts)  20 us
    dot_general x4, matrix products, query_scores(): jnp.einsum('gqhe,gnkhe->ghqnk', query_blk, key_blk, preferred_element_typ...  15.7 us
    all_to_all x1, blocking collectives, body(): lax.all_to_all(packed, 'head', split_axis=1, concat_axis=0, tiled=True)  12.6 us
    reshape x4, local copies, waits for them, and re-layouts, query_scores(): return scores.reshape(scores.shape[0], scores.shape[1], scores.shape[2], -1)  12.5 us
  transfers between devices with their start and end apart: 6, of which 4 were waited for; matrix products, arithmetic and copies ran while one was open for 10% of the time, Pallas kernels for 0%

commit v1 on v0

--- a/solution.py
+++ b/solution.py
@@ -58,7 +58,11 @@
     packed_heads = lax.all_to_all(packed, "head", split_axis=1, concat_axis=0, tiled=True)
     queries = packed_heads[:, :, :HD]
     pair_local = packed_heads[:, :, HD:]
-    pair_all = lax.all_gather(pair_local, "seq", axis=0, tiled=True)
+    peers = lax.axis_size("seq")
+    repeats = [peers if d == 0 else 1 for d in range(pair_local.ndim)]
+    pair_all = lax.all_to_all(
+        jnp.tile(pair_local, repeats), "seq", split_axis=0, concat_axis=0, tiled=True
+    )
     pair_table = pair_all.reshape(blocks_all, BLK, local_heads, 2 * HD)
     query_blocks = queries.reshape(local_blocks, BLK, local_heads, HD)
 

time: 561 us -> 597 us (1.064)
  local copies, waits for them, and re-layouts: 90.9 us -> 104 us
  waiting for transfers between devices: 348 us -> 357 us
  starting transfers between devices: 16.3 us -> 24.9 us
    all_to_all x0 -> x1, waiting for transfers between devices: none -> 47.8 us  [body(): lax.all_to_all(jnp.tile(pair_local, repeats), 'seq', split_axis=0, concat...]
    all_gather x1 -> x0, waiting for transfers between devices: 36.5 us -> none  [body(): pair_all = lax.all_gather(pair_local, 'seq', axis=0, tiled=True)]
    unnamed x33 -> x36, local copies, waits for them, and re-layouts: 5.97 us -> 22.3 us
    all_to_all x0 -> x1, starting transfers between devices: none -> 8.61 us  [body(): lax.all_to_all(jnp.tile(pair_local, repeats), 'seq', split_axis=0, concat...]
  transfers between devices with their start and end apart: 6 -> 6, of which waited for: 4 -> 4; matrix products, arithmetic and copies ran while one was open for 10% -> 11% of each run, Pallas kernels for 0% -> 0%
where the time goes in v1:
time: 597 us; the launch traced here: 594 us
  waiting for transfers between devices  357 us (60%)
  local copies, waits for them, and re-layouts  104 us (17%)
  other arithmetic  45.7 us (8%)
  matrix products  35.1 us (6%)
  starting transfers between devices  24.9 us (4%)
  between operations  14.3 us (2%)
  blocking collectives  12.6 us (2%)
    psum x1, waiting for transfers between devices, body(): lax.psum((local_qkv, local_out), ('dp', 'seq', 'head'))  263 us
    all_to_all x1, waiting for transfers between devices, body(): lax.all_to_all(jnp.tile(pair_local, repeats), 'seq', split_axis=0, concat...  47.8 us
    reduce_scatter x1, waiting for transfers between devices, body(): lax.psum_scatter(pair_sums.reshape(seq_length, local_heads, 2 * HD), 'seq...  41.2 us
    unnamed x36, local copies, waits for them, and re-layouts  22.3 us
    scatter-add x2, other arithmetic, scatter_step(): carried = carried.at[key_rows.reshape(-1)].add(both_parts)  20.1 us
    dot_general x4, matrix products, query_scores(): jnp.einsum('gqhe,gnkhe->ghqnk', query_blk, key_blk, preferred_element_typ...  15.6 us
    all_to_all x1, blocking collectives, body(): lax.all_to_all(packed, 'head', split_axis=1, concat_axis=0, tiled=True)  12.6 us
    reshape x4, local copies, waits for them, and re-layouts, query_scores(): return scores.reshape(scores.shape[0], scores.shape[1], scores.shape[2], -1)  12.4 us
  transfers between devices with their start and end apart: 6, of which 4 were waited for; matrix products, arithmetic and copies ran while one was open for 11% of the time, Pallas kernels for 0%

profile of v1, /device:TPU:2, one launch (start us, length us, event | category | flops | bytes accessed | tf_op | source)
XLA Modules:
  0.0 594.4 jit_solution(9020734415513466413)
XLA Ops:
  10.5 12.6 %all_to_all.68 = bf16[128,8,192]{0,2,1:T(8,128)(2,1)S(1)} all-to-all(bf16[128,8,192]{0,2,1:T(8,128)(2,1)S(1)} %bitcast.275), channel_id=1, replica_groups=mesh['dp'=4,'seq'=8,'head'=8] {'head'}, dimensions={1} | all-to-all | bytes 786432 | tf_op jit(solution)/shard_map/all_to_all | solution.py:58
  25.4 4.4 reduce.9
  29.9 5.8 reshape.399
  35.7 8.6 %all-to-all-start.1 = ((bf16[8,2,65536]{2,1,0:T(2,128)(2,1)}), bf16[8,2,65536]{2,1,0:T(2,128)(2,1)}, u32[]{:S(2)}, u32[]{:S(2)}) async-start(bf16[8,2,65536]{2,1,0:T(2,128)(2,1)} %reshape.399), calls=%async_computation.1 | async-start | bytes 4194304 | tf_op jit(solution)/shard_map/all_to_all | solution.py:63
  46.3 47.8 %all-to-all-done.1 = bf16[8,2,65536]{2,1,0:T(2,128)(2,1)} async-done(((bf16[8,2,65536]{2,1,0:T(2,128)(2,1)}), bf16[8,2,65536]{2,1,0:T(2,128)(2,1)}, u32[]{:S(2)}, u32[]{:S(2)}) %all-to-all-start.1) | async-done | bytes 2097184 | tf_op jit(solution)/shard_map/all_to_all | solution.py:63
  94.1 4.8 all-to-all-start.3
  98.9 6.8 %reshape.400 = bf16[8192,1,128]{2,1,0:T(2,128)(2,1)} reshape(bf16[8,2,65536]{2,1,0:T(2,128)(2,1)} %all-to-all-done.1) | data formatting | bytes 4194304
  105.7 3.8 copy.165
  110.1 40.2 %while.24 = (s32[]{:T(128)}, bf16[2,4,128,1,64]{2,4,1,3,0:T(8,128)(2,1)}, f32[2,4,1,128]{3,1,2,0:T(4,128)}, s32[2,4,9]{2,1,0:T(4,128)S(1)}, bf16[64,128,1,128]{3...) while((s32[]{:T(128)}, ...), condition=%wide.region_4.7_spmd, body=%wide.region_1.6_spmd.sunk | while | flops 156931296 | bytes 39141280 | solution.py:83
  111.5 3.4 gather_fusion
  118.7 3.6 fusion.80
  124.1 3.1 copy.182
  131.6 3.4 gather_fusion
  138.8 3.6 fusion.80
  144.2 3.1 copy.182
  154.4 86.1 %while.25 = (s32[]{:T(128)}, f32[64,128,1,128]{3,1,0,2:T(8,128)}, bf16[2,4,128,1,64]{2,4,1,3,0:T(8,128)(2,1)}, s32[2,4,9]{2,1,0:T(4,128)S(1)}, bf16[2,4,128,1,64...) while((s32[]{:T(128)}, f32[64,128,1,128]{3,1,0,2:T(8,128)}, ...), condition=%wide.region_8.11_spmd, body=%wide.region_6.10_spmd.sunk | while | flops 385783744 | bytes 64560684 | solution.py:148
  170.8 4.2 select_add_fusion.3
  175.0 3.1 copy.184
  178.1 2.5 fusion.94
  184.3 3.1 copy.186
  187.4 10.1 %scatter_fusion = f32[64,128,128]{2,1,0:T(8,128)} fusion(f32[64,128,128]{2,1,0:T(8,128)} %bitcast.266, s32[36]{0:T(128)S(1)} %copy-done.24, f32[36,128,128]{2,1,0:T(8,128)} %bitcast.260), kind=kCustom, calls=%fused_computation.4.clone.1 | custom fusion | flops 589824 | bytes 7078032 | tf_op jit(solution)/shard_map/while/body/eval_jaxpr/scatter-add | solution.py:144
  214.0 4.2 select_add_fusion.3
  218.1 3.1 copy.184
  221.2 2.5 fusion.94
  227.4 3.1 copy.186
  230.5 10.0 %scatter_fusion = f32[64,128,128]{2,1,0:T(8,128)} fusion(f32[64,128,128]{2,1,0:T(8,128)} %bitcast.266, s32[36]{0:T(128)S(1)} %copy-done.24, f32[36,128,128]{2,1,0:T(8,128)} %bitcast.260), kind=kCustom, calls=%fused_computation.4.clone.1 | custom fusion | flops 589824 | bytes 7078032 | tf_op jit(solution)/shard_map/while/body/eval_jaxpr/scatter-add | solution.py:144
  245.1 5.7 all-to-all-start.2
  251.1 41.2 %reduce-scatter.2.cloned.1.call-done = f32[1024,1,128]{2,1,0:T(1,128)} async-done(((f32[8192,1,128]{2,1,0:T(1,128)}), f32[1024,1,128]{2,1,0:T(1,128)}) %reduce-scatter.2.cloned.1.call-update) | async-done | bytes 524304 | tf_op jit(solution)/shard_map/reduce_scatter | solution.py:149
  295.7 4.0 reduce.11
  301.1 5.7 all-to-all-start.4
  308.8 4.7 all-to-all-done.4
  320.8 263.4 %all-reduce.3.cloned.1.call-done = (f32[512,1536]{0,1:T(8,128)}, f32[512,512]{0,1:T(8,128)}) async-done(((f32[512,1536]{0,1:T(8,128)}, f32[512,512]{0,1:T(8,128)}), (f32[512,1536]{0,1:T(8,128)}, f32[512,512]{0,1:T(8,128)})) %all-reduce.3.cloned.1.call-update) | async-done | bytes 4194320 | tf_op jit(solution)/shard_map/psum | solution.py:164
  (220 shorter events, 94.0 us)
Async XLA Ops:
  35.7 8.6 %copy-start.25 = (s32[1,64,9]{1,0,2:T(1,128)S(1)}, s32[1,64,9]{1,0,2:T(1,128)}, u32[]{:S(2)}) copy-start(s32[1,64,9]{1,0,2:T(1,128)} %param.17) | copy-start | bytes 6916
  35.7 8.8 %copy-start.6 = (bf16[512,512]{1,0:T(8,128)(2,1)S(1)}, bf16[512,512]{1,0:T(8,128)(2,1)}, u32[]{:S(2)}) copy-start(bf16[512,512]{1,0:T(8,128)(2,1)} %param.19) | copy-start | bytes 1572868
  35.7 8.8 %copy-start.17 = (bf16[1,128,512]{2,1,0:T(8,128)(2,1)S(1)}, bf16[1,128,512]{2,1,0:T(8,128)(2,1)}, u32[]{:S(2)}) copy-start(bf16[1,128,512]{2,1,0:T(8,128)(2,1)} %param.21) | copy-start | bytes 393220
  35.7 9.9 %copy-start.28 = (f32[8]{0:T(128)S(1)}, f32[8]{0:T(128)}, u32[]{:S(2)}) copy-start(f32[8]{0:T(128)} %param.20) | copy-start | bytes 100
  35.7 10.5 %copy-start.3 = (s32[1,8192]{1,0:T(1,128)S(1)}, s32[1,8192]{1,0:T(1,128)}, u32[]{:S(2)}) copy-start(s32[1,8192]{1,0:T(1,128)} %param.16) | copy-start | bytes 98308
  35.7 58.4 %all-to-all-start.1 = ((bf16[8,2,65536]{2,1,0:T(2,128)(2,1)}), bf16[8,2,65536]{2,1,0:T(2,128)(2,1)}, u32[]{:S(2)}, u32[]{:S(2)}) async-start(bf16[8,2,65536]{2,1,0:T(2,128)(2,1)} %reshape.399), calls=%async_computation.1 | async-start | bytes 4194304 | tf_op jit(solution)/shard_map/all_to_all | solution.py:63
  94.1 56.3 %all-to-all-start.3 = ((bf16[128,8,64]{0,2,1:T(8,128)(2,1)}), bf16[128,8,64]{0,2,1:T(8,128)(2,1)S(1)}, u32[]{:S(2)}, u32[]{:S(2)}) async-start(bf16[128,8,64]{0,2,1:T(8,128)(2,1)} %bitcast.51), calls=%async_computation.3 | async-start | bytes 262144 | tf_op jit(solution)/shard_map/all_to_all | solution.py:94
  98.9 193.4 %reduce-scatter.2.cloned.1.call-start = ((), (), s32[]{:S(2)}) async-start(), calls=%async_computation.6 | async-start | bytes 4718592 | tf_op jit(solution)/shard_map/reduce_scatter | solution.py:149
  118.7 5.4 copy-start.22
  124.1 3.1 copy-start.23
  124.1 3.1 copy-start.10
  138.8 5.4 copy-start.22
  144.2 3.1 copy-start.23
  144.2 3.1 copy-start.10
  154.4 2.6 copy-start.20
  154.4 6.5 %copy-start.8 = (bf16[2,4,128,1,64]{2,4,1,3,0:T(8,128)(2,1)}, bf16[2,4,128,1,64]{2,4,1,3,0:T(8,128)(2,1)S(1)}, u32[]{:S(2)}) copy-start(bf16[2,4,128,1,64]{2,4,1,3,0:T(8,128)(2,1)S(1)} %get-tuple-element.517) | copy-start | bytes 393220 | tf_op jit(solution)/shard_map/while
  178.1 2.5 copy-start.1
  182.3 2.0 copy-start.15
  184.3 3.1 copy-start.24
  187.4 10.1 %copy-start.21 = (f32[2,4,1,128]{3,1,2,0:T(4,128)S(1)}, f32[2,4,1,128]{3,1,2,0:T(4,128)}, u32[]{:S(2)}) copy-start(f32[2,4,1,128]{3,1,2,0:T(4,128)} %copy-done.20) | copy-start | bytes 12292 | tf_op jit(solution)/shard_map/while
  197.6 2.6 copy-start.20
  197.6 6.5 %copy-start.8 = (bf16[2,4,128,1,64]{2,4,1,3,0:T(8,128)(2,1)}, bf16[2,4,128,1,64]{2,4,1,3,0:T(8,128)(2,1)S(1)}, u32[]{:S(2)}) copy-start(bf16[2,4,128,1,64]{2,4,1,3,0:T(8,128)(2,1)S(1)} %get-tuple-element.517) | copy-start | bytes 393220 | tf_op jit(solution)/shard_map/while
  221.2 2.5 copy-start.1
  227.4 3.1 copy-start.24
  230.5 10.0 %copy-start.21 = (f32[2,4,1,128]{3,1,2,0:T(4,128)S(1)}, f32[2,4,1,128]{3,1,2,0:T(4,128)}, u32[]{:S(2)}) copy-start(f32[2,4,1,128]{3,1,2,0:T(4,128)} %copy-done.20) | copy-start | bytes 12292 | tf_op jit(solution)/shard_map/while
  241.5 9.3 %copy-start.16 = (bf16[2,4,128,1,64]{2,4,1,3,0:T(8,128)(2,1)S(1)}, bf16[2,4,128,1,64]{2,4,1,3,0:T(8,128)(2,1)}, u32[]{:S(2)}) copy-start(bf16[2,4,128,1,64]{2,4,1,3,0:T(8,128)(2,1)} %get-tuple-element.119) | copy-start | bytes 393220
  245.1 56.0 %all-to-all-start.2 = ((bf16[8,2,4096]{2,1,0:T(2,128)(2,1)}), bf16[8,2,4096]{2,1,0:T(2,128)(2,1)S(1)}, u32[]{:S(2)}, u32[]{:S(2)}) async-start(bf16[8,2,4096]{2,1,0:T(2,128)(2,1)} %reshape.401), calls=%async_computation.2 | async-start | bytes 262144 | tf_op jit(solution)/shard_map/all_to_all | solution.py:88
  295.7 11.8 %copy-start.18 = (bf16[1,128,512]{2,1,0:T(8,128)(2,1)S(1)}, bf16[1,128,512]{2,1,0:T(8,128)(2,1)}, u32[]{:S(2)}) copy-start(bf16[1,128,512]{2,1,0:T(8,128)(2,1)} %param.21) | copy-start | bytes 393220
  301.1 12.4 %all-to-all-start.4 = ((bf16[8,2,12288]{2,1,0:T(2,128)(2,1)}), bf16[8,2,12288]{2,1,0:T(2,128)(2,1)S(1)}, u32[]{:S(2)}, u32[]{:S(2)}) async-start(bf16[8,2,12288]{2,1,0:T(2,128)(2,1)} %reshape.403), calls=%async_computation.5 | async-start | bytes 786432 | tf_op jit(solution)/shard_map/all_to_all | solution.py:156
  306.8 277.4 %all-reduce.3.cloned.1.call-start = ((), (), s32[]{:S(2)}) async-start(), calls=%async_computation.7 | async-start | bytes 8388608 | tf_op jit(solution)/shard_map/psum | solution.py:164
  308.8 6.2 %copy-start.13 = (bf16[1,128,512]{2,1,0:T(8,128)(2,1)S(1)}, bf16[1,128,512]{2,1,0:T(8,128)(2,1)}, u32[]{:S(2)}) copy-start(bf16[1,128,512]{2,1,0:T(8,128)(2,1)} %param.15) | copy-start | bytes 393220
  308.8 6.2 %copy-start.27 = (f32[128]{0:T(128)S(1)}, f32[128]{0:T(128)}, u32[]{:S(2)}) copy-start(f32[128]{0:T(128)} %copy-done.26) | copy-start | bytes 1540
  (19 other events, 21.8 us)
Sparse Core Ops, SparseCore 0:
  240.7 51.5 reduce-scatter.1
  317.5 266.6 all-reduce.2
